TPU v7x, 256 devices: a whole 4x4x8 slice. The times are simulated.
256 devices in a mesh: dp: 4 (over y), fsdp: 8 (over z), tensor: 8 (over x, core).
Axes of the slice: x: 4, y: 4, z: 8, core: 2. Of those that a mesh axis runs over, the one named last changes fastest.
Arguments:
- momentum: bfloat16 [4, 8192, 8192], P('dp', 'fsdp', 'tensor'), may hold values from -24 to 24
- gradient: bfloat16 [4, 8192, 8192], P('dp', 'fsdp', 'tensor'), may hold values from -4 to 4
- factor: float32 [8192, 256], P('tensor'), may hold values from -6 to 6
Outputs:
- new_momentum: float32 [4, 8192, 8192], P('dp', 'fsdp', 'tensor')
- step_direction: bfloat16 [8192, 8192], P('fsdp', 'tensor')
- new_factor: float32 [8192, 256], P('tensor')
All inputs are finite; a program needn't handle non-finite values.
Results may differ from a plain program's by a relative error of at most 0.0065.
Values may be sent and summed in bfloat16 or wider, within the bound.
A program may use at most 64 MiB of HBM per device.

v0:
```python
import jax
import jax.numpy as jnp
from jax import lax
from jax.sharding import PartitionSpec as P

ROWS = 8192
COLS = 8192
RANK = 256


def orthonormal(rows_part, gram):
    lower = jnp.linalg.cholesky(gram)
    return jax.scipy.linalg.solve_triangular(lower, rows_part.T, lower=True).T


def transposed_product(block, ortho_low):
    return lax.dot_general(
        block, ortho_low, (((0,), (0,)), ((), ())), preferred_element_type=jnp.float32
    )


def local(momentum, gradient, factor):
    highest = lax.Precision.HIGHEST
    replicas = lax.axis_size("dp")
    moment = momentum[0]
    change = gradient[0]
    factor_low = factor.astype(jnp.bfloat16)
    partial_left = jnp.dot(moment, factor_low, preferred_element_type=jnp.float32)
    partial_left = partial_left + jnp.dot(change, factor_low, preferred_element_type=jnp.float32)
    left = lax.psum(partial_left, ("dp", "tensor")) / replicas
    gram = lax.psum(jnp.dot(left.T, left, precision=highest), "fsdp")
    ortho_low = orthonormal(left, gram).astype(jnp.bfloat16)
    partial_right = transposed_product(moment, ortho_low) + transposed_product(change, ortho_low)
    right = lax.psum(partial_right, ("dp", "fsdp")) / replicas
    square_sums = lax.psum(jnp.sum(right * right, axis=0), "tensor")
    new_factor = right / jnp.sqrt(square_sums / COLS + 1e-06)
    right_low = right.astype(jnp.bfloat16)
    feedback = jnp.dot(ortho_low, right_low.T, preferred_element_type=jnp.float32)
    new_momentum = (moment.astype(jnp.float32) + change.astype(jnp.float32) - 0.05 * feedback)[None]
    step_scale = jnp.sqrt(jnp.float32(ROWS / RANK))
    factor_next_low = new_factor.astype(jnp.bfloat16)
    step_direction = (
        step_scale * jnp.dot(ortho_low, factor_next_low.T, preferred_element_type=jnp.float32)
    ).astype(jnp.bfloat16)
    return (new_momentum, step_direction, new_factor)


def solution(mesh):
    in_specs = (P("dp", "fsdp", "tensor"), P("dp", "fsdp", "tensor"), P("tensor", None))
    out_specs = (P("dp", "fsdp", "tensor"), P("fsdp", "tensor"), P("tensor", None))
    return jax.shard_map(local, mesh=mesh, in_specs=in_specs, out_specs=out_specs, check_vma=False)
```

profile of v0, /device:TPU:1, one launch (start us, length us, event | category | flops | bytes accessed | tf_op | source)
XLA Modules:
  0.0 455.1 jit_solution(12589717732364756060)
XLA Ops:
  7.2 0.0 copy-start.1
  7.2 0.0 all-reduce.5.cloned.1.call-start
  7.2 2.7 fusion.2
  10.0 0.0 copy-done.7
  10.0 0.1 copy-done.1
  10.0 1.7 fusion.8
  11.7 0.0 all-reduce.5.cloned.1.call-update
  11.7 0.0 all-reduce.7.cloned.1.call-start
  11.8 119.2 %all-reduce.5.cloned.1.call-done = f32[1024,256]{1,0:T(8,128)} async-done(((f32[1024,256]{1,0:T(8,128)}), f32[1024,256]{1,0:T(8,128)}) %all-reduce.5.cloned.1.call-update) | async-done | bytes 1048592 | tf_op jit(solution)/shard_map/psum | solution.py:30
  131.0 4.2 fusion.17
  135.2 0.0 all-reduce.7.cloned.1.call-update
  135.2 0.2 all-reduce.9.cloned.1.call-start
  135.5 0.1 multiply_bitcast_fusion
  135.5 67.4 %all-reduce.7.cloned.1.call-done = f32[256,256]{0,1:T(8,128)} async-done(((f32[256,256]{0,1:T(8,128)}), f32[256,256]{0,1:T(8,128)}) %all-reduce.7.cloned.1.call-update) | async-done | bytes 262160 | tf_op jit(solution)/shard_map/psum | solution.py:31
  203.0 1.1 copy.7
  204.1 1.0 fusion.24
  205.1 11.7 %cholesky.50 = f32[128,128]{1,0:T(8,128)S(1)} custom-call(f32[128,128]{1,0:T(8,128)S(1)} %cholesky.118), custom_call_target="Cholesky" | custom-call | tf_op jit(solution)/shard_map/jit(cholesky)/cholesky | solution.py:12
  216.8 9.8 %custom-call.15 = f32[1,128,128]{1,2,0:T(8,128)S(1)} custom-call(f32[1,128,128]{2,1,0:T(8,128)S(1)} %get-tuple-element.24), custom_call_target="InvertDiagBlocksLowerTriangular" | custom-call | tf_op jit(solution)/shard_map/jit(cholesky)/cholesky | solution.py:12
  226.7 0.2 constant_dynamic-update-slice_fusion.1
  226.9 0.3 convolution_subtract_fusion.1
  227.1 11.7 %cholesky.105 = f32[128,128]{1,0:T(8,128)S(1)} custom-call(f32[128,128]{1,0:T(8,128)S(1)} %convolution_subtract_fusion.1), custom_call_target="Cholesky" | custom-call | tf_op jit(solution)/shard_map/jit(cholesky)/cholesky | solution.py:12
  238.9 0.6 compare_reduce_fusion
  240.8 0.7 select_select_fusion
  241.6 0.1 triangular_solve.57
  241.6 5.8 %while.1 = (s32[]{:T(128)}, f32[256,256]{1,0:T(8,128)}, s32[2,2]{1,0:T(2,128)S(1)}, f32[2,128,128]{2,1,0:T(8,128)S(1)}, s32[]{:T(128)}) while((s32[]{:T(128)}, f32[256,256]{1,0:T(8,128)}, s32[2,2]{1,0:T(2,128)S(1)}, f32[2,128,128]{2,1,0:T(8,128)S(1)}, s32[]{:T(128)}) %tuple.28), condition=%wide.while_cond, body=%wide.while_body.sunk | while | flops 2 | bytes 131189 | solution.py:13
  241.6 0.6 fusion.40
  242.2 2.3 bitcast_dynamic-update-slice_fusion.2
  244.6 0.6 fusion.40
  245.2 2.3 bitcast_dynamic-update-slice_fusion.2
  247.5 0.0 copy-start
  247.5 19.7 %custom-call.16 = f32[2,128,128]{1,2,0:T(8,128)S(1)} custom-call(f32[2,128,128]{2,1,0:T(8,128)S(1)} %get-tuple-element.10), custom_call_target="InvertDiagBlocksLowerTriangular" | custom-call | tf_op jit(solution)/shard_map/jit(_solve_triangular)/triangular_solve | solution.py:13
  267.2 0.6 fusion.34
  267.8 1.8 convolution_subtract_fusion
  269.7 0.0 copy-start.2
  269.7 0.6 convolution_convert_fusion
  270.3 0.9 fusion
  271.3 1.9 fusion.14
  273.2 0.0 all-reduce.9.cloned.1.call-update
  273.3 149.4 %all-reduce.9.cloned.1.call-done = f32[1024,256]{1,0:T(8,128)} async-done(((f32[1024,256]{1,0:T(8,128)}), f32[1024,256]{1,0:T(8,128)}) %all-reduce.9.cloned.1.call-update) | async-done | bytes 1048592 | tf_op jit(solution)/shard_map/psum | solution.py:34
  422.6 1.4 multiply_reduce_fusion
  424.0 17.3 %psum.31 = f32[256]{0:T(256)S(1)} all-reduce(f32[256]{0:T(256)S(1)} %multiply_reduce_fusion), channel_id=1, replica_groups=mesh['dp'=4,'fsdp'=8,'tensor'=8] {'tensor'}, use_global_device_ids=true, to_apply=%region_8.9 | all-reduce | flops 256 | bytes 2048 | tf_op jit(solution)/shard_map/psum | solution.py:35
  441.3 1.3 multiply_divide_fusion
  442.6 0.0 copy-start.6
  442.6 0.0 copy-start.3
  442.7 2.1 multiply_convert_fusion
  444.8 0.3 copy-done.3
  445.0 0.6 copy-done.4
  445.6 2.9 subtract_bitcast_fusion
  (16 shorter events, 0.1 us)
Async XLA Ops:
  7.2 2.8 copy-start.7
  7.2 2.9 copy-start.1
  7.2 123.8 %all-reduce.5.cloned.1.call-start = ((), (), s32[]{:S(2)}) async-start(), calls=%async_computation | async-start | bytes 2097152 | tf_op jit(solution)/shard_map/psum | solution.py:30
  11.7 191.2 %all-reduce.7.cloned.1.call-start = ((), (), s32[]{:S(2)}) async-start(), calls=%async_computation.1 | async-start | bytes 524288 | tf_op jit(solution)/shard_map/psum | solution.py:31
  131.0 4.4 copy-start.5
  135.2 287.4 %all-reduce.9.cloned.1.call-start = ((), (), s32[]{:S(2)}) async-start(), calls=%async_computation.2 | async-start | bytes 2097152 | tf_op jit(solution)/shard_map/psum | solution.py:34
  247.5 22.9 %copy-start = (bf16[1,1024,1024]{2,1,0:T(8,128)(2,1)S(1)}, bf16[1,1024,1024]{2,1,0:T(8,128)(2,1)}, u32[]{:S(2)}) copy-start(bf16[1,1024,1024]{2,1,0:T(8,128)(2,1)} %param.4) | copy-start | bytes 6291460
  269.7 1.6 copy-start.2
  442.6 6.0 %copy-start.6 = (f32[1024,256]{1,0:T(8,128)}, f32[1024,256]{1,0:T(8,128)S(1)}, u32[]{:S(2)}) copy-start(f32[1024,256]{1,0:T(8,128)S(1)} %multiply_divide_fusion) | copy-start | bytes 3145732
  442.6 2.4 copy-start.3
  442.7 3.0 copy-start.4
Sparse Core Ops, SparseCore 0:
  11.9 119.1 all-reduce.4
  135.3 67.5 all-reduce.6
  273.4 149.1 all-reduce.8
where the time goes:
time: 456 us; the launch traced here: 455 us
  waiting for transfers between devices  336 us (74%)
  other arithmetic  58.1 us (13%)
  matrix products  20.1 us (4%)
  blocking collectives  17.3 us (4%)
  between operations  15.3 us (3%)
  local copies, waits for them, and re-layouts  7.94 us (2%)
    psum x1, waiting for transfers between devices, local(): right = lax.psum(partial_right, ('dp', 'fsdp')) / replicas  149 us
    psum x1, waiting for transfers between devices, local(): left = lax.psum(partial_left, ('dp', 'tensor')) / replicas  119 us
    psum x1, waiting for transfers between devices, local(): gram = lax.psum(jnp.dot(left.T, left, precision=highest), 'fsdp')  67.4 us
    another operation x6, other arithmetic, orthonormal(): lower = jnp.linalg.cholesky(gram)  33.9 us
    another operation x3, other arithmetic, orthonormal(): return jax.scipy.linalg.solve_triangular(lower, rows_part.T, lower=True).T  20.4 us
    psum x1, blocking collectives, local(): square_sums = lax.psum(jnp.sum(right * right, axis=0), 'tensor')  17.3 us
  transfers between devices with their start and end apart: 3, of which 3 were waited for; matrix products, arithmetic and copies ran while one was open for 0% of the time, Pallas kernels for 0%

commit v1 on v0

--- a/solution.py
+++ b/solution.py
@@ -31,7 +31,7 @@
     gram = lax.psum(jnp.dot(left.T, left, precision=highest), "fsdp")
     ortho_low = orthonormal(left, gram).astype(jnp.bfloat16)
     partial_right = transposed_product(moment, ortho_low) + transposed_product(change, ortho_low)
-    right = lax.psum(partial_right, ("dp", "fsdp")) / replicas
+    right = lax.psum(lax.psum(partial_right, "fsdp"), "dp") / replicas
     square_sums = lax.psum(jnp.sum(right * right, axis=0), "tensor")
     new_factor = right / jnp.sqrt(square_sums / COLS + 1e-06)
     right_low = right.astype(jnp.bfloat16)

time: 456 us -> 433 us (0.950)
  waiting for transfers between devices: 336 us -> 316 us
    psum x1 -> x2, waiting for transfers between devices: 149 us -> 130 us  [local(): right = lax.psum(lax.psum(partial_right, 'fsdp'), 'dp') / replicas]
  transfers between devices with their start and end apart: 3 -> 4, of which waited for: 3 -> 4; matrix products, arithmetic and copies ran while one was open for 0% -> 0% of each run, Pallas kernels for 0% -> 0%
where the time goes in v1:
time: 433 us; the launch traced here: 432 us
  waiting for transfers between devices  316 us (73%)
  other arithmetic  58.1 us (13%)
  matrix products  20.1 us (5%)
  between operations  15.3 us (4%)
  blocking collectives  14.3 us (3%)
  local copies, waits for them, and re-layouts  7.94 us (2%)
    psum x2, waiting for transfers between devices, local(): right = lax.psum(lax.psum(partial_right, 'fsdp'), 'dp') / replicas  130 us
    psum x1, waiting for transfers between devices, local(): left = lax.psum(partial_left, ('dp', 'tensor')) / replicas  119 us
    psum x1, waiting for transfers between devices, local(): gram = lax.psum(jnp.dot(left.T, left, precision=highest), 'fsdp')  67.4 us
    another operation x6, other arithmetic, orthonormal(): lower = jnp.linalg.cholesky(gram)  33.9 us
    another operation x3, other arithmetic, orthonormal(): return jax.scipy.linalg.solve_triangular(lower, rows_part.T, lower=True).T  20.4 us
    psum x1, blocking collectives, local(): square_sums = lax.psum(jnp.sum(right * right, axis=0), 'tensor')  14.3 us
  transfers between devices with their start and end apart: 4, of which 4 were waited for; matrix products, arithmetic and copies ran while one was open for 0% of the time, Pallas kernels for 0%

profile of v1, /device:TPU:1, one launch (start us, length us, event | category | flops | bytes accessed | tf_op | source)
XLA Modules:
  0.0 432.5 jit_solution(70751014315420243)
XLA Ops:
  7.2 0.0 copy-start.1
  7.2 0.0 all-reduce.6.cloned.1.call-start
  7.2 2.7 fusion.2
  10.0 0.1 copy-done.1
  10.0 1.7 fusion.8
  11.7 0.0 all-reduce.6.cloned.1.call-update
  11.7 0.0 all-reduce.8.cloned.1.call-start
  11.8 119.2 %all-reduce.6.cloned.1.call-done = f32[1024,256]{1,0:T(8,128)} async-done(((f32[1024,256]{1,0:T(8,128)}), f32[1024,256]{1,0:T(8,128)}) %all-reduce.6.cloned.1.call-update) | async-done | bytes 1048592 | tf_op jit(solution)/shard_map/psum | solution.py:30
  131.0 4.2 fusion.17
  135.2 0.0 all-reduce.8.cloned.1.call-update
  135.2 0.2 all-reduce.10.cloned.1.call-start
  135.5 0.1 multiply_bitcast_fusion
  135.5 67.4 %all-reduce.8.cloned.1.call-done = f32[256,256]{0,1:T(8,128)} async-done(((f32[256,256]{0,1:T(8,128)}), f32[256,256]{0,1:T(8,128)}) %all-reduce.8.cloned.1.call-update) | async-done | bytes 262160 | tf_op jit(solution)/shard_map/psum | solution.py:31
  203.0 1.1 copy.7
  204.1 1.0 fusion.24
  205.1 11.7 %cholesky.50 = f32[128,128]{1,0:T(8,128)S(1)} custom-call(f32[128,128]{1,0:T(8,128)S(1)} %cholesky.118), custom_call_target="Cholesky" | custom-call | tf_op jit(solution)/shard_map/jit(cholesky)/cholesky | solution.py:12
  216.8 9.8 %custom-call.15 = f32[1,128,128]{1,2,0:T(8,128)S(1)} custom-call(f32[1,128,128]{2,1,0:T(8,128)S(1)} %get-tuple-element.24), custom_call_target="InvertDiagBlocksLowerTriangular" | custom-call | tf_op jit(solution)/shard_map/jit(cholesky)/cholesky | solution.py:12
  226.7 0.2 constant_dynamic-update-slice_fusion.1
  226.9 0.3 convolution_subtract_fusion.1
  227.1 11.7 %cholesky.105 = f32[128,128]{1,0:T(8,128)S(1)} custom-call(f32[128,128]{1,0:T(8,128)S(1)} %convolution_subtract_fusion.1), custom_call_target="Cholesky" | custom-call | tf_op jit(solution)/shard_map/jit(cholesky)/cholesky | solution.py:12
  238.9 0.6 compare_reduce_fusion
  240.8 0.7 select_select_fusion
  241.6 0.1 triangular_solve.57
  241.6 5.8 %while.1 = (s32[]{:T(128)}, f32[256,256]{1,0:T(8,128)}, s32[2,2]{1,0:T(2,128)S(1)}, f32[2,128,128]{2,1,0:T(8,128)S(1)}, s32[]{:T(128)}) while((s32[]{:T(128)}, f32[256,256]{1,0:T(8,128)}, s32[2,2]{1,0:T(2,128)S(1)}, f32[2,128,128]{2,1,0:T(8,128)S(1)}, s32[]{:T(128)}) %tuple.28), condition=%wide.while_cond, body=%wide.while_body.sunk | while | flops 2 | bytes 131189 | solution.py:13
  241.6 0.6 fusion.40
  242.2 2.3 bitcast_dynamic-update-slice_fusion.2
  244.6 0.6 fusion.40
  245.2 2.3 bitcast_dynamic-update-slice_fusion.2
  247.5 0.0 copy-start
  247.5 19.7 %custom-call.16 = f32[2,128,128]{1,2,0:T(8,128)S(1)} custom-call(f32[2,128,128]{2,1,0:T(8,128)S(1)} %get-tuple-element.10), custom_call_target="InvertDiagBlocksLowerTriangular" | custom-call | tf_op jit(solution)/shard_map/jit(_solve_triangular)/triangular_solve | solution.py:13
  267.2 0.6 fusion.34
  267.8 1.8 convolution_subtract_fusion
  269.7 0.0 copy-start.2
  269.7 0.6 convolution_convert_fusion
  270.3 0.9 fusion
  271.3 1.9 fusion.14
  273.2 0.0 all-reduce.10.cloned.1.call-update
  273.3 0.0 all-reduce.12.cloned.1.call-start
  273.3 75.2 %all-reduce.10.cloned.1.call-done = f32[1024,256]{1,0:T(8,128)} async-done(((f32[1024,256]{1,0:T(8,128)}), f32[1024,256]{1,0:T(8,128)}) %all-reduce.10.cloned.1.call-update) | async-done | bytes 1048592 | tf_op jit(solution)/shard_map/psum | solution.py:34
  348.5 0.0 all-reduce.12.cloned.1.call-update
  348.6 54.4 %all-reduce.12.cloned.1.call-done = f32[1024,256]{1,0:T(8,128)} async-done(((f32[1024,256]{1,0:T(8,128)}), f32[1024,256]{1,0:T(8,128)}) %all-reduce.12.cloned.1.call-update) | async-done | bytes 1048592 | tf_op jit(solution)/shard_map/psum | solution.py:34
  403.0 1.4 multiply_reduce_fusion
  404.4 14.3 %psum.39 = f32[256]{0:T(256)S(1)} all-reduce(f32[256]{0:T(256)S(1)} %multiply_reduce_fusion), channel_id=1, replica_groups=mesh['dp'=4,'fsdp'=8,'tensor'=8] {'tensor'}, use_global_device_ids=true, to_apply=%region_9.10 | all-reduce | flops 256 | bytes 2048 | tf_op jit(solution)/shard_map/psum | solution.py:35
  418.7 1.3 multiply_divide_fusion
  420.0 2.1 multiply_convert_fusion
  422.1 0.3 copy-done.3
  422.4 0.6 copy-done.4
  423.0 2.9 subtract_bitcast_fusion
  (19 shorter events, 0.2 us)
Async XLA Ops:
  7.2 2.8 copy-start.7
  7.2 2.9 copy-start.1
  7.2 123.8 %all-reduce.6.cloned.1.call-start = ((), (), s32[]{:S(2)}) async-start(), calls=%async_computation | async-start | bytes 2097152 | tf_op jit(solution)/shard_map/psum | solution.py:30
  11.7 191.2 %all-reduce.8.cloned.1.call-start = ((), (), s32[]{:S(2)}) async-start(), calls=%async_computation.1 | async-start | bytes 524288 | tf_op jit(solution)/shard_map/psum | solution.py:31
  131.0 4.4 %copy-start.5 = (f32[1024,256]{1,0:T(8,128)S(1)}, f32[1024,256]{1,0:T(8,128)}, u32[]{:S(2)}) copy-start(f32[1024,256]{1,0:T(8,128)} %all-reduce.6.cloned.1.call-done) | copy-start | bytes 3145732
  135.2 213.3 %all-reduce.10.cloned.1.call-start = ((), (), s32[]{:S(2)}) async-start(), calls=%async_computation.2 | async-start | bytes 2097152 | tf_op jit(solution)/shard_map/psum | solution.py:34
  247.5 22.9 %copy-start = (bf16[1,1024,1024]{2,1,0:T(8,128)(2,1)S(1)}, bf16[1,1024,1024]{2,1,0:T(8,128)(2,1)}, u32[]{:S(2)}) copy-start(bf16[1,1024,1024]{2,1,0:T(8,128)(2,1)} %param.4) | copy-start | bytes 6291460
  269.7 1.6 copy-start.2
  273.3 129.7 %all-reduce.12.cloned.1.call-start = ((), (), s32[]{:S(2)}) async-start(), calls=%async_computation.3 | async-start | bytes 2097152 | tf_op jit(solution)/shard_map/psum | solution.py:34
  420.0 6.0 %copy-start.6 = (f32[1024,256]{1,0:T(8,128)}, f32[1024,256]{1,0:T(8,128)S(1)}, u32[]{:S(2)}) copy-start(f32[1024,256]{1,0:T(8,128)S(1)} %multiply_divide_fusion) | copy-start | bytes 3145732
  420.0 2.4 copy-start.3
  420.0 3.0 copy-start.4
Sparse Core Ops, SparseCore 0:
  11.9 119.1 all-reduce.5
  135.3 67.5 all-reduce.7
  273.4 75.1 all-reduce.9
  350.8 52.1 all-reduce.11

commit v2 on v0

--- a/solution.py
+++ b/solution.py
@@ -31,7 +31,7 @@
     gram = lax.psum(jnp.dot(left.T, left, precision=highest), "fsdp")
     ortho_low = orthonormal(left, gram).astype(jnp.bfloat16)
     partial_right = transposed_product(moment, ortho_low) + transposed_product(change, ortho_low)
-    right = lax.psum(partial_right, ("dp", "fsdp")) / replicas
+    right = jnp.sum(lax.all_gather(partial_right, ("dp", "fsdp")), axis=0) / replicas
     square_sums = lax.psum(jnp.sum(right * right, axis=0), "tensor")
     new_factor = right / jnp.sqrt(square_sums / COLS + 1e-06)
     right_low = right.astype(jnp.bfloat16)

time: 456 us -> 574 us (1.26)
  waiting for transfers between devices: 336 us -> 423 us
  local copies, waits for them, and re-layouts: 7.94 us -> 37.1 us
  other arithmetic: 58.1 us -> 64.5 us
    all_gather x0 -> x1, waiting for transfers between devices: none -> 236 us  [local(): lax.all_gather(partial_right, ('dp', 'fsdp'))]
    psum x1 -> x0, waiting for transfers between devices: 149 us -> none  [local(): right = lax.psum(partial_right, ('dp', 'fsdp')) / replicas]
    unnamed x16 -> x17, local copies, waits for them, and re-layouts: 0.96 us -> 29.1 us
    reduce_sum x0 -> x1, other arithmetic: none -> 8.43 us  [local(): jnp.sum(lax.all_gather(partial_right, ('dp', 'fsdp')), axis=0) / replicas]
where the time goes in v2:
time: 574 us
  waiting for transfers between devices  423 us (74%)
  other arithmetic  64.5 us (11%)
  local copies, waits for them, and re-layouts  37.1 us (6%)
  matrix products  20.4 us (4%)
  between operations  15.3 us (3%)
  blocking collectives  13.3 us (2%)
    all_gather x1, waiting for transfers between devices, local(): lax.all_gather(partial_right, ('dp', 'fsdp'))  236 us
    psum x1, waiting for transfers between devices, local(): left = lax.psum(partial_left, ('dp', 'tensor')) / replicas  119 us
    psum x1, waiting for transfers between devices, local(): gram = lax.psum(jnp.dot(left.T, left, precision=highest), 'fsdp')  67.4 us
    another operation x6, other arithmetic, orthonormal(): lower = jnp.linalg.cholesky(gram)  34 us
    unnamed x17, local copies, waits for them, and re-layouts  29.1 us
    another operation x3, other arithmetic, orthonormal(): return jax.scipy.linalg.solve_triangular(lower, rows_part.T, lower=True).T  20.7 us
    psum x1, blocking collectives, local(): square_sums = lax.psum(jnp.sum(right * right, axis=0), 'tensor')  13.3 us
  transfers between devices with their start and end apart: 3, of which 3 were waited for; matrix products, arithmetic and copies ran while one was open for 0% of the time, Pallas kernels for 0%

profile of v2, /device:TPU:1, one launch (start us, length us, event | category | flops | bytes accessed | tf_op | source)
XLA Modules:
  0.0 573.6 jit_solution(11318824392923860030)
XLA Ops:
  7.2 0.0 copy-start.1
  7.2 0.0 all-reduce.4.cloned.1.call-start
  7.2 2.7 fusion.2
  10.0 0.0 copy-done.7
  10.0 0.1 copy-done.1
  10.0 1.7 fusion.8
  11.7 0.0 all-reduce.4.cloned.1.call-update
  11.7 0.0 all-reduce.6.cloned.1.call-start
  11.8 119.2 %all-reduce.4.cloned.1.call-done = f32[1024,256]{1,0:T(8,128)} async-done(((f32[1024,256]{1,0:T(8,128)}), f32[1024,256]{1,0:T(8,128)}) %all-reduce.4.cloned.1.call-update) | async-done | bytes 1048592 | tf_op jit(solution)/shard_map/psum | solution.py:30
  131.0 4.2 fusion.17
  135.2 0.0 all-reduce.6.cloned.1.call-update
  135.2 0.2 all-gather.3.cloned.1.call-start
  135.5 0.1 multiply_bitcast_fusion
  135.5 67.4 %all-reduce.6.cloned.1.call-done = f32[256,256]{0,1:T(8,128)} async-done(((f32[256,256]{0,1:T(8,128)}), f32[256,256]{0,1:T(8,128)}) %all-reduce.6.cloned.1.call-update) | async-done | bytes 262160 | tf_op jit(solution)/shard_map/psum | solution.py:31
  203.0 1.1 copy.9
  204.1 1.0 fusion.24
  205.1 11.7 %cholesky.50 = f32[128,128]{1,0:T(8,128)S(1)} custom-call(f32[128,128]{1,0:T(8,128)S(1)} %cholesky.118), custom_call_target="Cholesky" | custom-call | tf_op jit(solution)/shard_map/jit(cholesky)/cholesky | solution.py:12
  216.8 9.8 %custom-call.15 = f32[1,128,128]{1,2,0:T(8,128)S(1)} custom-call(f32[1,128,128]{2,1,0:T(8,128)S(1)} %get-tuple-element.24), custom_call_target="InvertDiagBlocksLowerTriangular" | custom-call | tf_op jit(solution)/shard_map/jit(cholesky)/cholesky | solution.py:12
  226.7 0.2 constant_dynamic-update-slice_fusion.1
  226.9 0.3 convolution_subtract_fusion.1
  227.1 11.7 %cholesky.105 = f32[128,128]{1,0:T(8,128)S(1)} custom-call(f32[128,128]{1,0:T(8,128)S(1)} %convolution_subtract_fusion.1), custom_call_target="Cholesky" | custom-call | tf_op jit(solution)/shard_map/jit(cholesky)/cholesky | solution.py:12
  238.9 0.7 compare_reduce_fusion
  241.0 0.1 triangular_solve.57
  241.1 5.5 while.1
  241.3 0.6 fusion.40
  241.8 2.1 bitcast_dynamic-update-slice_fusion.2
  243.9 0.6 fusion.40
  244.5 2.1 bitcast_dynamic-update-slice_fusion.2
  246.6 20.6 %custom-call.16 = f32[2,128,128]{1,2,0:T(8,128)S(1)} custom-call(f32[2,128,128]{2,1,0:T(8,128)} %get-tuple-element.10), custom_call_target="InvertDiagBlocksLowerTriangular" | custom-call | tf_op jit(solution)/shard_map/jit(_solve_triangular)/triangular_solve | solution.py:13
  267.2 0.6 fusion.34
  267.9 0.0 copy-start.3
  267.9 1.0 convolution_subtract_fusion
  268.9 0.0 copy-start.2
  268.9 0.6 convolution_convert_fusion
  269.5 0.7 fusion
  270.3 0.2 copy-done.2
  270.5 1.7 fusion.14
  272.2 0.0 all-gather.3.cloned.1.call-update
  272.2 235.9 %all-gather.3.cloned.1.call-done = f32[32768,256]{0,1:T(8,128)} async-done(((f32[1024,256]{0,1:T(8,128)}), f32[32768,256]{0,1:T(8,128)}) %all-gather.3.cloned.1.call-update) | async-done | bytes 33554448 | tf_op jit(solution)/shard_map/all_gather | solution.py:34
  508.1 28.8 %copy.12 = f32[32,8,32,1024]{3,2,1,0:T(8,128)S(1)} copy(f32[32,8,32,1024]{3,1,2,0:T(8,128)} %bitcast.62) | data formatting | bytes 67108864
  536.9 8.4 %bitcast_reduce_fusion = f32[1024,256]{0,1:T(8,128)} fusion(f32[32,8,32,1024]{3,2,1,0:T(8,128)S(1)} %copy.12), kind=kLoop, calls=%fused_computation.2 | loop fusion | flops 8126464 | bytes 34603008 | tf_op jit(solution)/shard_map/reduce_sum | solution.py:34
  545.3 1.6 copy.10
  546.9 0.2 multiply_reduce_fusion
  547.0 4.6 subtract_bitcast_fusion
  551.6 13.3 %psum.23 = f32[256]{0:T(256)S(1)} all-reduce(f32[256]{0:T(256)S(1)} %multiply_reduce_fusion), channel_id=1, replica_groups=mesh['dp'=4,'fsdp'=8,'tensor'=8] {'tensor'}, use_global_device_ids=true, to_apply=%region_8.9 | all-reduce | flops 256 | bytes 2048 | tf_op jit(solution)/shard_map/psum | solution.py:35
  564.9 0.1 multiply_divide_fusion
  565.0 0.0 copy-start.6
  565.0 2.1 multiply_convert_fusion
  (19 shorter events, 0.2 us)
Async XLA Ops:
  7.2 2.8 copy-start.7
  7.2 2.9 copy-start.1
  7.2 123.8 %all-reduce.4.cloned.1.call-start = ((), (), s32[]{:S(2)}) async-start(), calls=%async_computation | async-start | bytes 2097152 | tf_op jit(solution)/shard_map/psum | solution.py:30
  11.7 191.2 %all-reduce.6.cloned.1.call-start = ((), (), s32[]{:S(2)}) async-start(), calls=%async_computation.1 | async-start | bytes 524288 | tf_op jit(solution)/shard_map/psum | solution.py:31
  131.0 4.4 copy-start.5
  135.2 372.9 %all-gather.3.cloned.1.call-start = ((), (), s32[]{:S(2)}) async-start(), calls=%async_computation.2 | async-start | bytes 34603008 | tf_op jit(solution)/shard_map/all_gather | solution.py:34
  246.6 23.0 %copy-start = (bf16[1,1024,1024]{2,1,0:T(8,128)(2,1)S(1)}, bf16[1,1024,1024]{2,1,0:T(8,128)(2,1)}, u32[]{:S(2)}) copy-start(bf16[1,1024,1024]{2,1,0:T(8,128)(2,1)} %param.4) | copy-start | bytes 6291460
  267.9 2.4 copy-start.3
  268.9 1.6 copy-start.2
  551.6 13.4 %copy-start.4 = (bf16[128,1024]{1,0:T(8,128)(2,1)S(1)}, bf16[128,1024]{1,0:T(8,128)(2,1)}, u32[]{:S(2)}) copy-start(bf16[128,1024]{1,0:T(8,128)(2,1)} %copy-done.3) | copy-start | bytes 786436
  565.0 2.1 copy-start.6
Sparse Core Ops, SparseCore 0:
  11.9 119.1 all-reduce.3
  135.3 67.5 all-reduce.5
  272.3 235.7 all-gather.2
